TPU v7x, 32 devices: a whole 2x2x4 slice. The times are simulated.
32 devices in a mesh: dom: 2 (over y), dp: 16 (over z, x, core).
Axes of the slice: x: 2, y: 2, z: 4, core: 2. Of those that a mesh axis runs over, the one named last changes fastest.
Arguments:
- positions: float32 [1024, 128], P(('dom', 'dp')), may hold values from -6 to 6
- length_scale: float32 [1], replicated, may hold values from 16 to 128
- features: float32 [32768, 128], P('dp'), may hold values from -0.5 to 0.5
- labels: int32 [32768], P('dp'), may hold values 0 or 1
- batch_index: int32 [8192], P('dp'), may hold values from 0 to 2047
Outputs:
- moved: float32 [1024, 128], P(('dom', 'dp'))
- score: float32 [1024, 128], P(('dom', 'dp'))
Inputs may be any that keep to these rules, and one draw needn't show every extreme that they name: `batch_index`: an index into the 2048 feature rows of the same dp index.
All inputs are finite; a program needn't handle non-finite values. No bound on the sum of `labels` on one device may be relied on, other than what follows from the above.
Results may differ from a plain program's by a relative error of at most 0.0001.
Values sent between devices are 32-bit elements; how exact they have to be, the bound alone decides.
No kernel may reach another device: no remote copies, remote signals or barrier semaphores. Data moves between devices by JAX's collectives and lax.ppermute only.
A program may use at most 64 MiB of HBM per device.

v0:
```python
import math
import jax
import jax.numpy as jnp
from jax import lax
from jax.sharding import PartitionSpec as P

STEPS = 2
HIGH = lax.Precision.HIGHEST
STEP_SIZE = 2.0


def likelihood(block, rows, targets, scale):
    logits = jnp.dot(block, rows.T, precision=HIGH, preferred_element_type=jnp.float32)
    resid = targets[None, :] - jax.nn.sigmoid(logits)
    return jnp.dot(resid, rows, precision=HIGH, preferred_element_type=jnp.float32) * scale


def displace(aimed, sources, source_score, spread):
    square_a = jnp.sum(aimed * aimed, axis=1)
    square_b = jnp.sum(sources * sources, axis=1)
    inner = jnp.dot(aimed, sources.T, precision=HIGH, preferred_element_type=jnp.float32)
    dist = square_a[:, None] + square_b[None, :] - 2.0 * inner
    kernel = lax.rsqrt(1.0 + dist / spread)
    cubed = kernel * kernel * kernel
    drive = jnp.dot(kernel, source_score, precision=HIGH, preferred_element_type=jnp.float32)
    pulled = jnp.dot(cubed, sources, precision=HIGH, preferred_element_type=jnp.float32)
    return drive + (aimed * jnp.sum(cubed, axis=1)[:, None] - pulled) / spread


def shards(positions, length_scale, features, labels, batch_index):
    rows = features[batch_index]
    targets = labels[batch_index].astype(jnp.float32)
    scale = 1.0 / math.sqrt(batch_index.shape[0] * lax.axis_size("dp"))
    spread = length_scale[0]
    local_count = positions.shape[0]
    particle_total = local_count * lax.axis_size("dom") * lax.axis_size("dp")
    factor = STEP_SIZE / particle_total
    current = positions
    score = positions
    for iteration in range(STEPS):
        block = lax.all_gather(current, "dp", axis=0, tiled=True)
        gradient_block = lax.psum(likelihood(block, rows, targets, scale), "dp")
        score_block = gradient_block - block
        place = lax.axis_index("dp") * local_count
        score = lax.dynamic_slice_in_dim(score_block, place, local_count, 0)
        aimed_all = lax.all_gather(current, "dom", axis=0, tiled=True)
        moves = lax.psum_scatter(
            displace(aimed_all, block, score_block, spread), "dom", scatter_dimension=0, tiled=True
        )
        current = current + factor * moves
    return (current, score)


def solution(mesh):
    placed = (P(("dom", "dp"), None), P(), P("dp", None), P("dp"), P("dp"))
    return jax.shard_map(
        shards,
        mesh=mesh,
        in_specs=placed,
        out_specs=(P(("dom", "dp"), None), P(("dom", "dp"), None)),
        check_vma=False,
    )
```

profile of v0, /device:TPU:0, one launch (start us, length us, event | category | flops | bytes accessed | tf_op | source)
XLA Modules:
  0.0 272.5 jit_solution(17130246005774058776)
XLA Ops:
  7.2 24.2 %all_gather.13 = f32[512,128]{1,0:T(8,128)S(1)} all-gather(f32[32,128]{1,0:T(8,128)} %param.5), channel_id=1, replica_groups=mesh['dom'=2,'dp'=16] {'dp'}, dimensions={0}, use_global_device_ids=true | all-gather | bytes 278528 | tf_op jit(solution)/shard_map/all_gather | solution.py:41
  31.5 1.0 gather_fusion.1
  32.5 3.1 %gather_fusion = s32[512]{0:T(512)S(1)} fusion(s32[2048]{0:T(1024)S(1)} %copy-done.1, s32[1024]{0:T(1024)S(1)} %pad_clamp_fusion), kind=kCustom, calls=%fused_computation | custom fusion | bytes 6144 | tf_op jit(solution)/shard_map/gather | solution.py:32
  35.7 1.1 fusion.4
  36.8 2.5 convolution_multiply_fusion.1
  39.6 0.5 copy-done.2
  40.1 4.4 %all_gather.12 = f32[64,128]{1,0:T(8,128)S(1)} all-gather(f32[32,128]{1,0:T(8,128)S(1)} %copy-done.2), channel_id=1, replica_groups=mesh['dom'=2,'dp'=16] {'dom'}, dimensions={0}, use_global_device_ids=true | all-gather | bytes 49152 | tf_op jit(solution)/shard_map/all_gather | solution.py:46
  45.3 0.5 fusion.22
  45.8 80.8 %all-reduce.3.cloned.1.call-done = f32[512,128]{1,0:T(8,128)} async-done(((f32[512,128]{1,0:T(8,128)}), f32[512,128]{1,0:T(8,128)}) %all-reduce.3.cloned.1.call-update) | async-done | bytes 262160 | tf_op jit(solution)/shard_map/psum | solution.py:42
  126.6 1.2 fusion.20
  127.8 0.9 fusion.19
  128.8 10.6 %reduce-scatter.3.cloned.1.call-done = f32[32,128]{1,0:T(8,128)} async-done(((f32[64,128]{1,0:T(8,128)}), f32[32,128]{1,0:T(8,128)}) %reduce-scatter.3.cloned.1.call-update) | async-done | bytes 16400 | tf_op jit(solution)/shard_map/reduce_scatter | solution.py:47
  139.4 0.7 multiply_add_fusion.1
  140.1 22.0 %all_gather.15 = f32[512,128]{1,0:T(8,128)S(1)} all-gather(f32[32,128]{1,0:T(8,128)S(1)} %multiply_add_fusion.1), channel_id=1, replica_groups=mesh['dom'=2,'dp'=16] {'dp'}, dimensions={0}, use_global_device_ids=true | all-gather | bytes 278528 | tf_op jit(solution)/shard_map/all_gather | solution.py:41
  162.1 1.1 fusion.7
  163.2 1.7 convolution_multiply_fusion
  165.0 4.4 %all_gather.14 = f32[64,128]{1,0:T(8,128)S(1)} all-gather(f32[32,128]{1,0:T(8,128)S(1)} %multiply_add_fusion.1), channel_id=1, replica_groups=mesh['dom'=2,'dp'=16] {'dom'}, dimensions={0}, use_global_device_ids=true | all-gather | bytes 49152 | tf_op jit(solution)/shard_map/all_gather | solution.py:46
  169.5 81.7 %all-reduce.5.cloned.1.call-done = f32[512,128]{1,0:T(8,128)} async-done(((f32[512,128]{1,0:T(8,128)}), f32[512,128]{1,0:T(8,128)}) %all-reduce.5.cloned.1.call-update) | async-done | bytes 262160 | tf_op jit(solution)/shard_map/psum | solution.py:42
  251.2 1.1 fusion.24
  252.3 0.5 fusion.23
  253.1 0.9 fusion.17
  254.0 0.6 constant_dynamic-slice_fusion
  254.6 10.0 %reduce-scatter.5.cloned.1.call-done = f32[32,128]{1,0:T(8,128)} async-done(((f32[64,128]{1,0:T(8,128)}), f32[32,128]{1,0:T(8,128)}) %reduce-scatter.5.cloned.1.call-update) | async-done | bytes 16400 | tf_op jit(solution)/shard_map/reduce_scatter | solution.py:47
  264.6 1.3 multiply_add_fusion
  (22 shorter events, 0.9 us)
Async XLA Ops:
  7.2 24.3 %copy-start = (f32[2048,128]{1,0:T(8,128)S(1)}, f32[2048,128]{1,0:T(8,128)}, u32[]{:S(2)}) copy-start(f32[2048,128]{1,0:T(8,128)} %param.7) | copy-start | bytes 3145732
  7.2 24.2 %copy-start.3 = (s32[512]{0:T(512)S(1)}, s32[512]{0:T(512)}, u32[]{:S(2)}) copy-start(s32[512]{0:T(512)} %param.9) | copy-start | bytes 6148
  7.2 119.4 %all-reduce.3.cloned.1.call-start = ((), (), s32[]{:S(2)}) async-start(), calls=%async_computation.2 | async-start | bytes 524288 | tf_op jit(solution)/shard_map/psum | solution.py:42
  31.4 1.1 copy-start.1
  39.4 0.7 copy-start.2
  39.4 100.0 %reduce-scatter.3.cloned.1.call-start = ((), (), s32[]{:S(2)}) async-start(), calls=%async_computation.3 | async-start | bytes 49152 | tf_op jit(solution)/shard_map/reduce_scatter | solution.py:47
  128.8 122.4 %all-reduce.5.cloned.1.call-start = ((), (), s32[]{:S(2)}) async-start(), calls=%async_computation.4 | async-start | bytes 524288 | tf_op jit(solution)/shard_map/psum | solution.py:42
  164.9 99.7 %reduce-scatter.5.cloned.1.call-start = ((), (), s32[]{:S(2)}) async-start(), calls=%async_computation.5 | async-start | bytes 49152 | tf_op jit(solution)/shard_map/reduce_scatter | solution.py:47
Sparse Core Ops, SparseCore 0:
  39.5 87.0 all-reduce.2
  128.9 10.4 reduce-scatter.2
  165.1 86.0 all-reduce.4
  254.1 10.4 reduce-scatter.4
where the time goes:
time: 273 us
  waiting for transfers between devices  183 us (67%)
  blocking collectives  55 us (20%)
  between operations  14.5 us (5%)
  matrix products  10.8 us (4%)
  local copies, waits for them, and re-layouts  5.33 us (2%)
  other arithmetic  3.51 us (1%)
    psum x2, waiting for transfers between devices, shards(): gradient_block = lax.psum(likelihood(block, rows, targets, scale), 'dp')  163 us
    all_gather x2, blocking collectives, shards(): block = lax.all_gather(current, 'dp', axis=0, tiled=True)  46.2 us
    reduce_scatter x2, waiting for transfers between devices, shards(): lax.psum_scatter(displace(aimed_all, block, score_block, spread), 'dom',...  20.6 us
    all_gather x2, blocking collectives, shards(): aimed_all = lax.all_gather(current, 'dom', axis=0, tiled=True)  8.8 us
  transfers between devices with their start and end apart: 4, of which 4 were waited for; matrix products, arithmetic and copies ran while one was open for 1% of the time, Pallas kernels for 0%

commit v1 on v0

--- a/solution.py
+++ b/solution.py
@@ -39,7 +39,9 @@
     score = positions
     for iteration in range(STEPS):
         block = lax.all_gather(current, "dp", axis=0, tiled=True)
-        gradient_block = lax.psum(likelihood(block, rows, targets, scale), "dp")
+        part = likelihood(block, rows, targets, scale)
+        parts = lax.all_gather(part, "dp")
+        gradient_block = jnp.sum(parts, axis=0)
         score_block = gradient_block - block
         place = lax.axis_index("dp") * local_count
         score = lax.dynamic_slice_in_dim(score_block, place, local_count, 0)

time: 273 us -> 194 us (0.71)
  waiting for transfers between devices: 183 us -> 101 us
  other arithmetic: 3.51 us -> 8.06 us
    psum x2 -> x0, waiting for transfers between devices: 163 us -> none  [shards(): gradient_block = lax.psum(likelihood(block, rows, targets, scale), 'dp')]
    all_gather x0 -> x2, waiting for transfers between devices: none -> 84.2 us  [shards(): parts = lax.all_gather(part, 'dp')]
    reduce_sum x0 -> x2, other arithmetic: none -> 4.81 us  [shards(): gradient_block = jnp.sum(parts, axis=0)]
    reduce_scatter x2, waiting for transfers between devices: 20.6 us -> 16.6 us  [shards(): lax.psum_scatter(displace(aimed_all, block, score_block, spread), 'dom',...]
where the time goes in v1:
time: 194 us
  waiting for transfers between devices  101 us (52%)
  blocking collectives  55 us (28%)
  between operations  14.5 us (7%)
  matrix products  9.86 us (5%)
  other arithmetic  8.06 us (4%)
  local copies, waits for them, and re-layouts  5.05 us (3%)
    all_gather x2, waiting for transfers between devices, shards(): parts = lax.all_gather(part, 'dp')  84.2 us
    all_gather x2, blocking collectives, shards(): block = lax.all_gather(current, 'dp', axis=0, tiled=True)  46.2 us
    reduce_scatter x2, waiting for transfers between devices, shards(): lax.psum_scatter(displace(aimed_all, block, score_block, spread), 'dom',...  16.6 us
    all_gather x2, blocking collectives, shards(): aimed_all = lax.all_gather(current, 'dom', axis=0, tiled=True)  8.81 us
    reduce_sum x2, other arithmetic, shards(): gradient_block = jnp.sum(parts, axis=0)  4.81 us
    dot_general x2, matrix products, likelihood(): jnp.dot(resid, rows, precision=HIGH, preferred_element_type=jnp.float32)  4.2 us
  transfers between devices with their start and end apart: 4, of which 4 were waited for; matrix products, arithmetic and copies ran while one was open for 1% of the time, Pallas kernels for 0%

profile of v1, /device:TPU:0, one launch (start us, length us, event | category | flops | bytes accessed | tf_op | source)
XLA Modules:
  0.0 193.5 jit_solution(2082215944158865842)
XLA Ops:
  7.2 24.2 %all_gather.25 = f32[512,128]{1,0:T(8,128)S(1)} all-gather(f32[32,128]{1,0:T(8,128)} %param.5), channel_id=1, replica_groups=mesh['dom'=2,'dp'=16] {'dp'}, dimensions={0}, use_global_device_ids=true | all-gather | bytes 278528 | tf_op jit(solution)/shard_map/all_gather | solution.py:41
  31.4 0.7 compare_select_fusion
  32.1 1.0 gather_fusion.1
  33.2 3.4 %gather_fusion = s32[512]{0:T(512)S(1)} fusion(s32[2048]{0:T(1024)} %param.8, s32[1024]{0:T(1024)S(1)} %pad_clamp_fusion), kind=kCustom, calls=%fused_computation | custom fusion | bytes 6144 | tf_op jit(solution)/shard_map/gather | solution.py:32
  36.6 1.1 fusion.4
  37.7 2.5 %convolution_multiply_fusion.1 = f32[512,128]{1,0:T(8,128)} fusion(f32[512,512]{1,0:T(8,128)S(1)} %fusion.4, f32[512,128]{1,0:T(8,128)S(1)} %gather_fusion.1), kind=kOutput, calls=%fused_computation.13 | convolution fusion | flops 402718720 | bytes 1572864 | tf_op jit(solution)/shard_map/dot_general | solution.py:15
  41.0 4.4 %all_gather.24 = f32[64,128]{1,0:T(8,128)S(1)} all-gather(f32[32,128]{1,0:T(8,128)S(1)} %copy-done.1), channel_id=1, replica_groups=mesh['dom'=2,'dp'=16] {'dom'}, dimensions={0}, use_global_device_ids=true | all-gather | bytes 49152 | tf_op jit(solution)/shard_map/all_gather | solution.py:48
  45.6 0.5 fusion.22
  46.1 41.9 %all-gather.5.cloned.1.call-done = f32[8192,128]{1,0:T(8,128)} async-done(((f32[512,128]{1,0:T(8,128)}), f32[8192,128]{1,0:T(8,128)}) %all-gather.5.cloned.1.call-update) | async-done | bytes 4194320 | tf_op jit(solution)/shard_map/all_gather | solution.py:43
  88.1 2.4 %reduce_sum.74 = f32[512,128]{1,0:T(8,128)S(1)} reduce(f32[16,512,128]{2,1,0:T(8,128)} %bitcast.25, f32[]{:T(128)} %constant.10.clone.1), dimensions={0}, to_apply=%region_2.0 | reduce | flops 983040 | bytes 4456452 | tf_op jit(solution)/shard_map/reduce_sum | solution.py:44
  90.8 0.9 fusion.19
  91.7 8.6 %reduce-scatter.3.cloned.1.call-done = f32[32,128]{1,0:T(8,128)} async-done(((f32[64,128]{1,0:T(8,128)}), f32[32,128]{1,0:T(8,128)}) %reduce-scatter.3.cloned.1.call-update) | async-done | bytes 16400 | tf_op jit(solution)/shard_map/reduce_scatter | solution.py:49
  100.3 0.7 multiply_add_fusion.1
  101.1 22.0 %all_gather.29 = f32[512,128]{1,0:T(8,128)S(1)} all-gather(f32[32,128]{1,0:T(8,128)S(1)} %multiply_add_fusion.1), channel_id=1, replica_groups=mesh['dom'=2,'dp'=16] {'dp'}, dimensions={0}, use_global_device_ids=true | all-gather | bytes 278528 | tf_op jit(solution)/shard_map/all_gather | solution.py:41
  123.1 1.1 fusion.7
  124.2 1.7 convolution_multiply_fusion
  126.0 4.4 %all_gather.28 = f32[64,128]{1,0:T(8,128)S(1)} all-gather(f32[32,128]{1,0:T(8,128)S(1)} %multiply_add_fusion.1), channel_id=1, replica_groups=mesh['dom'=2,'dp'=16] {'dom'}, dimensions={0}, use_global_device_ids=true | all-gather | bytes 49152 | tf_op jit(solution)/shard_map/all_gather | solution.py:48
  130.5 42.3 %all-gather.7.cloned.1.call-done = f32[8192,128]{1,0:T(8,128)} async-done(((f32[512,128]{1,0:T(8,128)}), f32[8192,128]{1,0:T(8,128)}) %all-gather.7.cloned.1.call-update) | async-done | bytes 4194320 | tf_op jit(solution)/shard_map/all_gather | solution.py:43
  172.7 2.4 %reduce_sum.78 = f32[512,128]{1,0:T(8,128)S(1)} reduce(f32[16,512,128]{2,1,0:T(8,128)} %bitcast.24, f32[]{:T(128)} %constant.10.clone.1), dimensions={0}, to_apply=%region_7.0 | reduce | flops 983040 | bytes 4456452 | tf_op jit(solution)/shard_map/reduce_sum | solution.py:44
  175.3 0.5 fusion.23
  176.1 0.9 fusion.17
  177.0 0.6 constant_dynamic-slice_fusion
  177.6 8.0 %reduce-scatter.5.cloned.1.call-done = f32[32,128]{1,0:T(8,128)} async-done(((f32[64,128]{1,0:T(8,128)}), f32[32,128]{1,0:T(8,128)}) %reduce-scatter.5.cloned.1.call-update) | async-done | bytes 16400 | tf_op jit(solution)/shard_map/reduce_scatter | solution.py:49
  185.7 1.3 multiply_add_fusion
  (20 shorter events, 1.3 us)
Async XLA Ops:
  7.2 24.9 %copy-start = (f32[2048,128]{1,0:T(8,128)S(1)}, f32[2048,128]{1,0:T(8,128)}, u32[]{:S(2)}) copy-start(f32[2048,128]{1,0:T(8,128)} %param.7) | copy-start | bytes 3145732
  7.2 80.9 %all-gather.5.cloned.1.call-start = ((), (), s32[]{:S(2)}) async-start(), calls=%async_computation.4 | async-start | bytes 4456448 | tf_op jit(solution)/shard_map/all_gather | solution.py:43
  33.1 7.8 %copy-start.1 = (f32[32,128]{1,0:T(8,128)S(1)}, f32[32,128]{1,0:T(8,128)}, u32[]{:S(2)}) copy-start(f32[32,128]{1,0:T(8,128)} %param.5) | copy-start | bytes 49156
  40.2 60.1 %reduce-scatter.3.cloned.1.call-start = ((), (), s32[]{:S(2)}) async-start(), calls=%async_computation.2 | async-start | bytes 49152 | tf_op jit(solution)/shard_map/reduce_scatter | solution.py:49
  91.7 81.1 %all-gather.7.cloned.1.call-start = ((), (), s32[]{:S(2)}) async-start(), calls=%async_computation.5 | async-start | bytes 4456448 | tf_op jit(solution)/shard_map/all_gather | solution.py:43
  125.9 59.8 %reduce-scatter.5.cloned.1.call-start = ((), (), s32[]{:S(2)}) async-start(), calls=%async_computation.3 | async-start | bytes 49152 | tf_op jit(solution)/shard_map/reduce_scatter | solution.py:49
Sparse Core Ops, SparseCore 0:
  40.4 47.6 all-gather.4
  91.8 8.4 reduce-scatter.2
  126.0 46.6 all-gather.6
  177.1 8.4 reduce-scatter.4
